TPU v7x, 512 devices: a whole 4x8x8 slice. The times are simulated.
512 devices in a mesh: ctx: 128 (over z, y, core), tp: 4 (over x).
Axes of the slice: x: 4, y: 8, z: 8, core: 2. Of those that a mesh axis runs over, the one named last changes fastest.
Arguments:
- query: bfloat16 [32768, 4096], P('ctx', 'tp'), may hold values from -96 to 96
- key: bfloat16 [32768, 4096], P('ctx', 'tp'), may hold values from -4 to 4
- value: bfloat16 [32768, 4096], P('ctx', 'tp'), may hold values from -6 to 6
- xin: bfloat16 [32768, 4096], P('ctx', 'tp'), may hold values from -1 to 8
- gate_z: bfloat16 [32768, 4096], P('ctx', 'tp'), may hold values from -6 to 6
- w_bc: bfloat16 [4096, 32], P('tp'), may hold values from -1 to 1
- dt_low: bfloat16 [32768, 256], P('ctx'), may hold values from -4 to 9
- dt_proj: bfloat16 [256, 4096], P(None, 'tp'), may hold values from -3 to 3
- dt_bias: float32 [4096], P('tp'), may hold values from -20 to 0
- a_rate: float32 [16, 4096], P(None, 'tp'), may hold values from 1 to 16
- skip: float32 [4096], P('tp'), may hold values from 0.2 to 2
Outputs:
- attended: bfloat16 [32768, 4096], P('ctx', 'tp')
- mixed: bfloat16 [32768, 4096], P('ctx', 'tp')
All inputs are finite; a program needn't handle non-finite values.
Results may differ from a plain program's by a relative error of at most 0.0085.
Values may be sent and summed in bfloat16 or wider, within the bound.
No kernel may reach another device: no remote copies, remote signals or barrier semaphores. Data moves between devices by JAX's collectives and lax.ppermute only.
A program may use at most 128 MiB of HBM per device.

v0:
```python
import jax
import jax.numpy as jnp
from jax import lax
from jax.sharding import PartitionSpec as P

HD = 128
WINDOW = 2048
NS = 16


def passed_along(block, axis, distance):
    devices = range(lax.axis_size(axis))
    route = [(i - distance, i) for i in devices if i - distance in devices]
    return lax.ppermute(block, axis, route)


def entering(shard, axis, combine, identity):
    peers, here = (lax.axis_size(axis), lax.axis_index(axis))
    everything = jax.tree.map(lambda part: lax.all_gather(part, axis), shard)
    start = jax.tree.map(
        lambda part, zero: jnp.broadcast_to(jnp.asarray(zero, part.dtype), part.shape),
        shard,
        identity,
    )

    def step(k, before):
        reached = k < here
        new = combine(before, jax.tree.map(lambda part: part[k], everything))
        return jax.tree.map(lambda a, b: jnp.where(reached, a, b), new, before)

    return lax.fori_loop(0, peers, step, start)


def combine_states(earlier, later):
    return (earlier[0] * later[0], later[0] * earlier[1] + later[1])


def sweep_states(start_state, decay_rates, step_sizes, driven, b_rows, c_rows, with_output):
    tok_rows, channels = step_sizes.shape
    length = 32
    blocks = tok_rows // length
    inputs = (
        step_sizes.reshape(blocks, length, channels),
        driven.reshape(blocks, length, channels),
        b_rows.reshape(blocks, length, b_rows.shape[1]),
        c_rows.reshape(blocks, length, c_rows.shape[1]),
    )

    def advance(carried, block_in):
        sizes_block, drive_block, b_block, c_block = block_in
        outputs = []
        for offset in range(length):
            carried = (
                jnp.exp(-sizes_block[offset][None, :] * decay_rates) * carried
                + drive_block[offset][None, :] * b_block[offset][:, None]
            )
            if with_output:
                outputs.append(jnp.sum(c_block[offset][:, None] * carried, axis=0))
        if with_output:
            return (carried, jnp.stack(outputs))
        return (carried, None)

    last_state, produced = lax.scan(advance, start_state, inputs)
    if with_output:
        return (last_state, produced.reshape(tok_rows, channels))
    return (last_state, None)


def window_attention(query, pieces, place, reach):
    tok_rows = query.shape[0]
    ordered = jnp.concatenate(pieces[::-1], axis=1)
    key_pos = (place - reach) * tok_rows + jnp.arange(ordered.shape[1], dtype=jnp.int32)
    query_pos = place * tok_rows + jnp.arange(tok_rows, dtype=jnp.int32)
    allowed = (
        (key_pos[None, :] <= query_pos[:, None])
        & (key_pos[None, :] > query_pos[:, None] - WINDOW)
        & (key_pos[None, :] >= 0)
    )
    scale = HD ** (-0.5)
    heads_dev = query.shape[1] // HD
    results = []
    for head_num in range(heads_dev):
        column = slice(head_num * HD, (head_num + 1) * HD)
        scores = (
            lax.dot_general(
                query[:, column],
                ordered[0][:, column],
                (((1,), (1,)), ((), ())),
                preferred_element_type=jnp.float32,
            )
            * scale
        )
        masked = jnp.where(allowed, scores, -jnp.inf)
        row_max = jnp.max(masked, axis=1, keepdims=True)
        unscaled = jnp.where(allowed, jnp.exp(scores - row_max), 0.0)
        row_sum = jnp.sum(unscaled, axis=1, keepdims=True)
        probs = (unscaled / row_sum).astype(jnp.bfloat16)
        results.append(
            jnp.dot(probs, ordered[1][:, column], preferred_element_type=jnp.float32).astype(
                jnp.bfloat16
            )
        )
    return jnp.concatenate(results, axis=1)


def shards(query, key, value, xin, gate_z, w_bc, dt_low, dt_proj, dt_bias, a_rate, skip):
    tok_rows = query.shape[0]
    place = lax.axis_index("ctx")
    stacked = jnp.stack([key, value])
    reach = WINDOW // tok_rows
    pieces = [stacked]
    for distance in range(1, reach + 1):
        pieces.append(passed_along(stacked, "ctx", distance))
    partial_bc = jnp.dot(xin, w_bc, preferred_element_type=jnp.float32)
    summed_bc = lax.psum(partial_bc, "tp")
    b_rows = summed_bc[:, :NS]
    c_rows = summed_bc[:, NS:]
    step_sizes = jax.nn.softplus(
        jnp.dot(dt_low, dt_proj, preferred_element_type=jnp.float32) + dt_bias[None, :]
    )
    inputs_float = xin.astype(jnp.float32)
    driven = step_sizes * inputs_float
    zero_state = jnp.zeros((NS, step_sizes.shape[1]), jnp.float32)
    local_end, local_out = sweep_states(
        zero_state, a_rate, step_sizes, driven, b_rows, c_rows, False
    )
    through = jnp.sum(step_sizes, axis=0)
    decay_all = jnp.exp(-a_rate * through[None, :])
    prefix = entering(
        (decay_all, local_end),
        "ctx",
        combine_states,
        (jnp.ones_like(decay_all), jnp.zeros_like(local_end)),
    )
    incoming = prefix[1]
    attended = window_attention(query, pieces, place, reach)
    unused_state, outputs = sweep_states(incoming, a_rate, step_sizes, driven, b_rows, c_rows, True)
    mixed = (
        (outputs + skip[None, :] * inputs_float) * jax.nn.silu(gate_z.astype(jnp.float32))
    ).astype(jnp.bfloat16)
    return (attended, mixed)


def solution(mesh):
    in_specs = (
        P("ctx", "tp"),
        P("ctx", "tp"),
        P("ctx", "tp"),
        P("ctx", "tp"),
        P("ctx", "tp"),
        P("tp", None),
        P("ctx", None),
        P(None, "tp"),
        P("tp"),
        P(None, "tp"),
        P("tp"),
    )
    out_specs = (P("ctx", "tp"), P("ctx", "tp"))
    return jax.shard_map(shards, mesh=mesh, in_specs=in_specs, out_specs=out_specs, check_vma=False)
```

profile of v0, /device:TPU:1, one launch (start us, length us, event | category | flops | bytes accessed | tf_op | source)
XLA Modules:
  0.0 662.3 jit_solution(11239584919717683615)
XLA Ops:
  8.6 14.5 %psum.7 = f32[256,32]{0,1:T(8,128)S(1)} all-reduce(f32[256,32]{0,1:T(8,128)S(1)} %fusion.264), channel_id=1, replica_groups=mesh['ctx'=128,'tp'=4] {'tp'}, use_global_device_ids=true, to_apply=%region_17.18 | all-reduce | flops 8192 | bytes 65536 | tf_op jit(solution)/shard_map/psum | solution.py:115
  23.8 2.5 convert_multiply_fusion.2
  26.3 38.5 %while.38 = (s32[]{:T(128)}, f32[16,1024]{1,0:T(8,128)}, f32[8,32,1024]{2,1,0:T(8,128)S(1)}, f32[16,1024]{1,0:T(8,128)S(1)}, f32[8,32,1024]{2,1,0:T(8,128)S(1)},...) while((s32[]{:T(128)}, f32[16,1024]{1,0:T(8,128)}, ...), condition=%wide.region_19.20_spmd.clone, body=%wide.region_18.19_spmd.clone.sunk | while | flops 2146338 | bytes 990295 | solution.py:63
  33.5 2.3 multiply_add_fusion.42
  38.4 2.3 multiply_add_fusion.42
  43.2 2.3 multiply_add_fusion.42
  48.1 2.3 multiply_add_fusion.42
  52.9 2.3 multiply_add_fusion.42
  67.5 8.1 %collective-permute-start = (bf16[2,256,1024]{2,1,0:T(8,128)(2,1)}, bf16[2,256,1024]{2,1,0:T(8,128)(2,1)}, u32[]{:S(2)}, u32[]{:S(2)}) collective-permute-start(bf16[2,256,1024]{2,1,0:T(8,128)(2,1)} %pad_maximum_fusion), channel_id=1, source_target_pairs={{0,32},{4,36},{8,40},{12,44},{16,48},{20,52},{24,56},{28,60},{32,6... | collective-permute-start | bytes 3145736 | tf_op jit(solution)/shard_map/ppermute | solution.py:14
  75.6 8.2 %collective-permute-start.1 = (bf16[2,256,1024]{2,1,0:T(8,128)(2,1)}, bf16[2,256,1024]{2,1,0:T(8,128)(2,1)}, u32[]{:S(2)}, u32[]{:S(2)}) collective-permute-start(bf16[2,256,1024]{2,1,0:T(8,128)(2,1)} %pad_maximum_fusion), channel_id=1, source_target_pairs={{0,28},{4,32},{8,36},{12,40},{16,44},{20,48},{24,52},{28,56},{32,6... | collective-permute-start | bytes 3145736 | tf_op jit(solution)/shard_map/ppermute | solution.py:14
  83.7 5.2 collective-permute-start.2
  91.2 5.2 collective-permute-start.4
  96.5 9.6 %collective-permute-done = bf16[2,256,1024]{2,1,0:T(8,128)(2,1)} collective-permute-done((bf16[2,256,1024]{2,1,0:T(8,128)(2,1)}, bf16[2,256,1024]{2,1,0:T(8,128)(2,1)}, u32[]{:S(2)}, u32[]{:S(2)}) %collective-permute-start) | collective-permute-done | bytes 1048608 | tf_op jit(solution)/shard_map/ppermute | solution.py:14
  106.0 27.5 %collective-permute-start.5 = (bf16[2,256,1024]{2,1,0:T(8,128)(2,1)}, bf16[2,256,1024]{2,1,0:T(8,128)(2,1)}, u32[]{:S(2)}, u32[]{:S(2)}) collective-permute-start(bf16[2,256,1024]{2,1,0:T(8,128)(2,1)} %pad_maximum_fusion), channel_id=1, source_target_pairs={{0,12},{4,16},{8,20},{12,24},{16,28},{20,32},{24,36},{28,40},{32,4... | collective-permute-start | bytes 3145736 | tf_op jit(solution)/shard_map/ppermute | solution.py:14
  133.7 31.2 %collective-permute-done.1 = bf16[2,256,1024]{2,1,0:T(8,128)(2,1)} collective-permute-done((bf16[2,256,1024]{2,1,0:T(8,128)(2,1)}, bf16[2,256,1024]{2,1,0:T(8,128)(2,1)}, u32[]{:S(2)}, u32[]{:S(2)}) %collective-permute-start.1) | collective-permute-done | bytes 1048608 | tf_op jit(solution)/shard_map/ppermute | solution.py:14
  166.2 66.4 %collective-permute-done.2 = bf16[2,256,1024]{2,1,0:T(8,128)(2,1)} collective-permute-done((bf16[2,256,1024]{2,1,0:T(8,128)(2,1)}, bf16[2,256,1024]{2,1,0:T(8,128)(2,1)}, u32[]{:S(2)}, u32[]{:S(2)}) %collective-permute-start.2) | collective-permute-done | bytes 1048608 | tf_op jit(solution)/shard_map/ppermute | solution.py:14
  232.6 60.1 %collective-permute-start.7 = (bf16[2,256,1024]{2,1,0:T(8,128)(2,1)}, bf16[2,256,1024]{2,1,0:T(8,128)(2,1)S(1)}, u32[]{:S(2)}, u32[]{:S(2)}) collective-permute-start(bf16[2,256,1024]{2,1,0:T(8,128)(2,1)} %pad_maximum_fusion), channel_id=1, source_target_pairs={{0,4},{4,8},{8,12},{12,16},{16,20},{20,24},{24,28},{28,32},{32,36}... | collective-permute-start | bytes 3145736 | tf_op jit(solution)/shard_map/ppermute | solution.py:14
  292.8 2.3 constant_dynamic-update-slice_fusion.8
  297.3 2.3 constant_dynamic-update-slice_fusion.6
  299.7 2.3 constant_dynamic-update-slice_fusion.5
  302.0 9.0 %collective-permute-done.4 = bf16[2,256,1024]{2,1,0:T(8,128)(2,1)} collective-permute-done((bf16[2,256,1024]{2,1,0:T(8,128)(2,1)}, bf16[2,256,1024]{2,1,0:T(8,128)(2,1)}, u32[]{:S(2)}, u32[]{:S(2)}) %collective-permute-start.4) | collective-permute-done | bytes 1048608 | tf_op jit(solution)/shard_map/ppermute | solution.py:14
  311.0 2.3 constant_dynamic-update-slice_fusion.4
  313.3 79.2 %collective-permute-done.5 = bf16[2,256,1024]{2,1,0:T(8,128)(2,1)} collective-permute-done((bf16[2,256,1024]{2,1,0:T(8,128)(2,1)}, bf16[2,256,1024]{2,1,0:T(8,128)(2,1)}, u32[]{:S(2)}, u32[]{:S(2)}) %collective-permute-start.5) | collective-permute-done | bytes 1048608 | tf_op jit(solution)/shard_map/ppermute | solution.py:14
  394.8 25.3 %collective-permute-done.6 = bf16[2,256,1024]{2,1,0:T(8,128)(2,1)S(1)} collective-permute-done((bf16[2,256,1024]{2,1,0:T(8,128)(2,1)}, bf16[2,256,1024]{2,1,0:T(8,128)(2,1)S(1)}, u32[]{:S(2)}, u32[]{:S(2)}) %collective-permute-start.6) | collective-permute-done | bytes 1048608 | tf_op jit(solution)/shard_map/ppermute | solution.py:14
  421.1 14.0 %collective-permute-done.7 = bf16[2,256,1024]{2,1,0:T(8,128)(2,1)S(1)} collective-permute-done((bf16[2,256,1024]{2,1,0:T(8,128)(2,1)}, bf16[2,256,1024]{2,1,0:T(8,128)(2,1)S(1)}, u32[]{:S(2)}, u32[]{:S(2)}) %collective-permute-start.7) | collective-permute-done | bytes 1048608 | tf_op jit(solution)/shard_map/ppermute | solution.py:14
  437.3 7.1 %slice_bitcast_fusion = (bf16[2304,1024]{1,0:T(8,128)(2,1)}, bf16[2304,1024]{1,0:T(8,128)(2,1)S(1)}) fusion(bf16[2,2304,1024]{2,1,0:T(8,128)(2,1)} %constant_dynamic-update-slice_fusion), kind=kLoop, calls=%fused_computation.478 | loop fusion | bytes 18874368 | tf_op jit(solution)/shard_map/squeeze | solution.py:99
  448.3 2.5 fusion.200
  452.2 4.0 fusion.199
  466.4 37.8 %all-gather.5.cloned.1.call-done = f32[2048,1024]{1,0:T(8,128)} async-done(((f32[16,1024]{1,0:T(8,128)}), f32[2048,1024]{1,0:T(8,128)}) %all-gather.5.cloned.1.call-update) | async-done | bytes 8388624 | tf_op jit(solution)/shard_map/all_gather | solution.py:19
  504.2 119.9 %while.39 = (s32[]{:T(128)}, f32[16,1024]{1,0:T(8,128)S(1)}, s32[]{:T(128)}, f32[128,16,1024]{2,1,0:T(8,128)}, f32[128,16,1024]{2,1,0:T(8,128)}, /*index=5*/s32[]{:T(128)}, s32[]{:T(128)}) while((s32[]{:T(128)}, f32[16,1024]{1,0:T(8,128)S(1)}, s32[]{:T(128)}, f32[128,16,1024]{2,1,0:T(8,128)}, f32[128,16,1024]{2,1,0:T(8,128)}, ...), condition=%wide.region_21.22_spmd.clone, body=%wide.region_20.21_spmd.clone.sunk | while | flops 65540 | bytes 262245 | solution.py:31
  624.1 28.7 %while.37 = (s32[]{:T(128)}, f32[16,1024]{1,0:T(8,128)S(1)}, f32[8,32,1024]{2,1,0:T(8,128)}, f32[8,32,1024]{2,1,0:T(8,128)S(1)}, f32[16,1024]{1,0:T(8,128)S(1)},...) while((s32[]{:T(128)}, f32[16,1024]{1,0:T(8,128)S(1)}, ...), condition=%wide.region_55.56_spmd, body=%wide.region_22.55_spmd.sunk | while | flops 4718625 | bytes 3357861 | solution.py:63
  652.8 2.6 fusion.227
  (387 shorter events, 203.2 us)
Async XLA Ops:
  7.2 16.6 %copy-start = (bf16[256,1024]{1,0:T(8,128)(2,1)S(1)}, bf16[256,1024]{1,0:T(8,128)(2,1)}, u32[]{:S(2)}) copy-start(bf16[256,1024]{1,0:T(8,128)(2,1)} %param.24) | copy-start | bytes 1572868
  7.2 459.2 %all-gather.7.cloned.1.call-start = ((), (), s32[]{:S(2)}) async-start(), calls=%async_computation.1 | async-start | bytes 8454144 | tf_op jit(solution)/shard_map/all_gather | solution.py:19
  7.2 19.1 %copy-start.2 = (f32[16,1024]{1,0:T(8,128)S(1)}, f32[16,1024]{1,0:T(8,128)}, u32[]{:S(2)}) copy-start(f32[16,1024]{1,0:T(8,128)} %param.26) | copy-start | bytes 196612
  26.3 40.0 %copy-start.4 = (bf16[256,1024]{1,0:T(8,128)(2,1)S(1)}, bf16[256,1024]{1,0:T(8,128)(2,1)}, u32[]{:S(2)}) copy-start(bf16[256,1024]{1,0:T(8,128)(2,1)} %param.19) | copy-start | bytes 1572868
  26.3 40.0 %copy-start.5 = (bf16[256,1024]{1,0:T(8,128)(2,1)S(1)}, bf16[256,1024]{1,0:T(8,128)(2,1)}, u32[]{:S(2)}) copy-start(bf16[256,1024]{1,0:T(8,128)(2,1)} %param.18) | copy-start | bytes 1572868
  64.9 68.7 %copy-start.7 = (f32[256,16]{0,1:T(8,128)S(1)}, f32[256,16]{0,1:T(8,128)}, u32[]{:S(2)}) copy-start(f32[256,16]{0,1:T(8,128)} %get-tuple-element.564) | copy-start | bytes 49156
  64.9 439.3 %all-gather.5.cloned.1.call-start = ((), (), s32[]{:S(2)}) async-start(), calls=%async_computation | async-start | bytes 8454144 | tf_op jit(solution)/shard_map/all_gather | solution.py:19
  67.5 38.6 %collective-permute-start = (bf16[2,256,1024]{2,1,0:T(8,128)(2,1)}, bf16[2,256,1024]{2,1,0:T(8,128)(2,1)}, u32[]{:S(2)}, u32[]{:S(2)}) collective-permute-start(bf16[2,256,1024]{2,1,0:T(8,128)(2,1)} %pad_maximum_fusion), channel_id=1, source_target_pairs={{0,32},{4,36},{8,40},{12,44},{16,48},{20,52},{24,56},{28,60},{32,6... | collective-permute-start | bytes 3145736 | tf_op jit(solution)/shard_map/ppermute | solution.py:14
  75.6 89.3 %collective-permute-start.1 = (bf16[2,256,1024]{2,1,0:T(8,128)(2,1)}, bf16[2,256,1024]{2,1,0:T(8,128)(2,1)}, u32[]{:S(2)}, u32[]{:S(2)}) collective-permute-start(bf16[2,256,1024]{2,1,0:T(8,128)(2,1)} %pad_maximum_fusion), channel_id=1, source_target_pairs={{0,28},{4,32},{8,36},{12,40},{16,44},{20,48},{24,52},{28,56},{32,6... | collective-permute-start | bytes 3145736 | tf_op jit(solution)/shard_map/ppermute | solution.py:14
  83.7 148.9 %collective-permute-start.2 = (bf16[2,256,1024]{2,1,0:T(8,128)(2,1)}, bf16[2,256,1024]{2,1,0:T(8,128)(2,1)}, u32[]{:S(2)}, u32[]{:S(2)}) collective-permute-start(bf16[2,256,1024]{2,1,0:T(8,128)(2,1)} %pad_maximum_fusion), channel_id=1, source_target_pairs={{0,24},{4,28},{8,32},{12,36},{16,40},{20,44},{24,48},{28,52},{32,5... | collective-permute-start | bytes 3145736 | tf_op jit(solution)/shard_map/ppermute | solution.py:14
  89.0 210.7 %collective-permute-start.3 = (bf16[2,256,1024]{2,1,0:T(8,128)(2,1)}, bf16[2,256,1024]{2,1,0:T(8,128)(2,1)}, u32[]{:S(2)}, u32[]{:S(2)}) collective-permute-start(bf16[2,256,1024]{2,1,0:T(8,128)(2,1)} %pad_maximum_fusion), channel_id=1, source_target_pairs={{0,20},{4,24},{8,28},{12,32},{16,36},{20,40},{24,44},{28,48},{32,5... | collective-permute-start | bytes 3145736 | tf_op jit(solution)/shard_map/ppermute | solution.py:14
  91.2 219.7 %collective-permute-start.4 = (bf16[2,256,1024]{2,1,0:T(8,128)(2,1)}, bf16[2,256,1024]{2,1,0:T(8,128)(2,1)}, u32[]{:S(2)}, u32[]{:S(2)}) collective-permute-start(bf16[2,256,1024]{2,1,0:T(8,128)(2,1)} %pad_maximum_fusion), channel_id=1, source_target_pairs={{0,16},{4,20},{8,24},{12,28},{16,32},{20,36},{24,40},{28,44},{32,4... | collective-permute-start | bytes 3145736 | tf_op jit(solution)/shard_map/ppermute | solution.py:14
  106.0 286.4 %collective-permute-start.5 = (bf16[2,256,1024]{2,1,0:T(8,128)(2,1)}, bf16[2,256,1024]{2,1,0:T(8,128)(2,1)}, u32[]{:S(2)}, u32[]{:S(2)}) collective-permute-start(bf16[2,256,1024]{2,1,0:T(8,128)(2,1)} %pad_maximum_fusion), channel_id=1, source_target_pairs={{0,12},{4,16},{8,20},{12,24},{16,28},{20,32},{24,36},{28,40},{32,4... | collective-permute-start | bytes 3145736 | tf_op jit(solution)/shard_map/ppermute | solution.py:14
  164.8 255.2 %collective-permute-start.6 = (bf16[2,256,1024]{2,1,0:T(8,128)(2,1)}, bf16[2,256,1024]{2,1,0:T(8,128)(2,1)S(1)}, u32[]{:S(2)}, u32[]{:S(2)}) collective-permute-start(bf16[2,256,1024]{2,1,0:T(8,128)(2,1)} %pad_maximum_fusion), channel_id=1, source_target_pairs={{0,8},{4,12},{8,16},{12,20},{16,24},{20,28},{24,32},{28,36},{32,40... | collective-permute-start | bytes 3145736 | tf_op jit(solution)/shard_map/ppermute | solution.py:14
  232.6 202.5 %collective-permute-start.7 = (bf16[2,256,1024]{2,1,0:T(8,128)(2,1)}, bf16[2,256,1024]{2,1,0:T(8,128)(2,1)S(1)}, u32[]{:S(2)}, u32[]{:S(2)}) collective-permute-start(bf16[2,256,1024]{2,1,0:T(8,128)(2,1)} %pad_maximum_fusion), channel_id=1, source_target_pairs={{0,4},{4,8},{8,12},{12,16},{16,20},{20,24},{24,28},{28,32},{32,36}... | collective-permute-start | bytes 3145736 | tf_op jit(solution)/shard_map/ppermute | solution.py:14
  437.3 7.1 %copy-start.6 = (bf16[256,1024]{1,0:T(8,128)(2,1)S(1)}, bf16[256,1024]{1,0:T(8,128)(2,1)}, u32[]{:S(2)}) copy-start(bf16[256,1024]{1,0:T(8,128)(2,1)} %param.17) | copy-start | bytes 1572868
  447.2 3.6 slice-start
  448.3 2.5 slice-start.1
  624.1 28.7 %copy-start.3 = (bf16[256,1024]{1,0:T(8,128)(2,1)S(1)}, bf16[256,1024]{1,0:T(8,128)(2,1)}, u32[]{:S(2)}) copy-start(bf16[256,1024]{1,0:T(8,128)(2,1)} %param.20) | copy-start | bytes 1572868
  624.1 28.7 %copy-start.8 = (f32[1024]{0:T(1024)S(1)}, f32[1024]{0:T(1024)}, u32[]{:S(2)}) copy-start(f32[1024]{0:T(1024)} %param.27) | copy-start | bytes 12292
  652.8 2.6 copy-start.1
Sparse Core Ops, SparseCore 0:
  65.0 344.9 all-gather.6
  413.1 90.9 all-gather.4
where the time goes:
time: 669 us; the launch traced here: 662 us
  waiting for transfers between devices  272 us (41%)
  other arithmetic  169 us (25%)
  starting transfers between devices  118 us (18%)
  local copies, waits for them, and re-layouts  49.5 us (7%)
  matrix products  20.8 us (3%)
  blocking collectives  14.5 us (2%)
  between operations  14.3 us (2%)
    ppermute x8, waiting for transfers between devices, passed_along(): return lax.ppermute(block, axis, route)  235 us
    ppermute x8, starting transfers between devices, passed_along(): return lax.ppermute(block, axis, route)  118 us
    select_n x128, other arithmetic, step(): return jax.tree.map(lambda a, b: jnp.where(reached, a, b), new, before)  117 us
    all_gather x2, waiting for transfers between devices, entering(): everything = jax.tree.map(lambda part: lax.all_gather(part, axis), shard)  37.8 us
    add x8, other arithmetic, advance(): jnp.exp(-sizes_block[offset][None, :] * decay_rates) * carried  18.2 us
    unnamed x32, local copies, waits for them, and re-layouts  17.1 us
    psum x1, blocking collectives, shards(): summed_bc = lax.psum(partial_bc, 'tp')  14.5 us
    reduce_sum x72, other arithmetic, advance(): outputs.append(jnp.sum(c_block[offset][:, None] * carried, axis=0))  14.1 us
  transfers between devices with their start and end apart: 10, of which 8 were waited for; matrix products, arithmetic and copies ran while one was open for 7% of the time, Pallas kernels for 0%

commit v1 on v0

--- a/solution.py
+++ b/solution.py
@@ -2,10 +2,16 @@
 import jax.numpy as jnp
 from jax import lax
 from jax.sharding import PartitionSpec as P
+from jax.lax import all_gather
 
 HD = 128
 WINDOW = 2048
 NS = 16
+
+
+def _clear_object(device_axis, mine):
+    state_next = all_gather(mine, device_axis).sum(axis=0)
+    return state_next
 
 
 def passed_along(block, axis, distance):
@@ -112,7 +118,7 @@
     for distance in range(1, reach + 1):
         pieces.append(passed_along(stacked, "ctx", distance))
     partial_bc = jnp.dot(xin, w_bc, preferred_element_type=jnp.float32)
-    summed_bc = lax.psum(partial_bc, "tp")
+    summed_bc = _clear_object("tp", partial_bc)
     b_rows = summed_bc[:, :NS]
     c_rows = summed_bc[:, NS:]
     step_sizes = jax.nn.softplus(

time: 669 us -> 667 us (level)
    psum x1 -> x0, blocking collectives: 14.5 us -> none  [shards(): summed_bc = lax.psum(partial_bc, 'tp')]
    all_gather x0 -> x1, blocking collectives: none -> 10.4 us  [_clear_object(): state_next = all_gather(mine, device_axis).sum(axis=0)]
where the time goes in v1:
time: 667 us; the launch traced here: 660 us
  waiting for transfers between devices  275 us (41%)
  other arithmetic  169 us (25%)
  starting transfers between devices  117 us (18%)
  local copies, waits for them, and re-layouts  49.6 us (7%)
  matrix products  20.7 us (3%)
  between operations  14.3 us (2%)
  blocking collectives  10.4 us (2%)
    ppermute x8, waiting for transfers between devices, passed_along(): return lax.ppermute(block, axis, route)  236 us
    select_n x128, other arithmetic, step(): return jax.tree.map(lambda a, b: jnp.where(reached, a, b), new, before)  117 us
    ppermute x8, starting transfers between devices, passed_along(): return lax.ppermute(block, axis, route)  117 us
    all_gather x2, waiting for transfers between devices, entering(): everything = jax.tree.map(lambda part: lax.all_gather(part, axis), shard)  38.6 us
    add x8, other arithmetic, advance(): jnp.exp(-sizes_block[offset][None, :] * decay_rates) * carried  18.2 us
    unnamed x32, local copies, waits for them, and re-layouts  17.1 us
    reduce_sum x72, other arithmetic, advance(): outputs.append(jnp.sum(c_block[offset][:, None] * carried, axis=0))  14.1 us
  transfers between devices with their start and end apart: 10, of which 8 were waited for; matrix products, arithmetic and copies ran while one was open for 7% of the time, Pallas kernels for 0%

profile of v1, /device:TPU:1, one launch (start us, length us, event | category | flops | bytes accessed | tf_op | source)
XLA Modules:
  0.0 659.6 jit_solution(5692601206210254011)
XLA Ops:
  8.6 10.4 %all-gather.1 = f32[1024,32]{0,1:T(8,128)S(1)} all-gather(f32[256,32]{0,1:T(8,128)S(1)} %fusion.264), channel_id=3, replica_groups=mesh['ctx'=128,'tp'=4] {'tp'}, dimensions={0}, use_global_device_ids=true | all-gather | bytes 163840 | tf_op jit(solution)/shard_map/all_gather | solution.py:13
  19.9 2.5 convert_multiply_fusion.2
  22.4 38.5 %while.38 = (s32[]{:T(128)}, f32[16,1024]{1,0:T(8,128)}, f32[8,32,1024]{2,1,0:T(8,128)S(1)}, f32[16,1024]{1,0:T(8,128)S(1)}, f32[8,32,1024]{2,1,0:T(8,128)S(1)},...) while((s32[]{:T(128)}, f32[16,1024]{1,0:T(8,128)}, ...), condition=%wide.region_19.20_spmd.clone, body=%wide.region_18.19_spmd.clone.sunk | while | flops 2146338 | bytes 990295 | solution.py:69
  29.6 2.3 multiply_add_fusion.42
  34.5 2.3 multiply_add_fusion.42
  39.3 2.3 multiply_add_fusion.42
  44.1 2.3 multiply_add_fusion.42
  49.0 2.3 multiply_add_fusion.42
  63.5 8.4 %collective-permute-start = (bf16[2,256,1024]{2,1,0:T(8,128)(2,1)}, bf16[2,256,1024]{2,1,0:T(8,128)(2,1)}, u32[]{:S(2)}, u32[]{:S(2)}) collective-permute-start(bf16[2,256,1024]{2,1,0:T(8,128)(2,1)} %pad_maximum_fusion), channel_id=1, source_target_pairs={{0,32},{4,36},{8,40},{12,44},{16,48},{20,52},{24,56},{28,60},{32,6... | collective-permute-start | bytes 3145736 | tf_op jit(solution)/shard_map/ppermute | solution.py:20
  72.0 7.3 %collective-permute-start.1 = (bf16[2,256,1024]{2,1,0:T(8,128)(2,1)}, bf16[2,256,1024]{2,1,0:T(8,128)(2,1)}, u32[]{:S(2)}, u32[]{:S(2)}) collective-permute-start(bf16[2,256,1024]{2,1,0:T(8,128)(2,1)} %pad_maximum_fusion), channel_id=1, source_target_pairs={{0,28},{4,32},{8,36},{12,40},{16,44},{20,48},{24,52},{28,56},{32,6... | collective-permute-start | bytes 3145736 | tf_op jit(solution)/shard_map/ppermute | solution.py:20
  79.3 5.3 collective-permute-start.2
  86.8 5.2 collective-permute-start.4
  92.0 10.6 %collective-permute-done = bf16[2,256,1024]{2,1,0:T(8,128)(2,1)} collective-permute-done((bf16[2,256,1024]{2,1,0:T(8,128)(2,1)}, bf16[2,256,1024]{2,1,0:T(8,128)(2,1)}, u32[]{:S(2)}, u32[]{:S(2)}) %collective-permute-start) | collective-permute-done | bytes 1048608 | tf_op jit(solution)/shard_map/ppermute | solution.py:20
  102.6 26.8 %collective-permute-start.5 = (bf16[2,256,1024]{2,1,0:T(8,128)(2,1)}, bf16[2,256,1024]{2,1,0:T(8,128)(2,1)}, u32[]{:S(2)}, u32[]{:S(2)}) collective-permute-start(bf16[2,256,1024]{2,1,0:T(8,128)(2,1)} %pad_maximum_fusion), channel_id=1, source_target_pairs={{0,12},{4,16},{8,20},{12,24},{16,28},{20,32},{24,36},{28,40},{32,4... | collective-permute-start | bytes 3145736 | tf_op jit(solution)/shard_map/ppermute | solution.py:20
  129.4 32.7 %collective-permute-done.1 = bf16[2,256,1024]{2,1,0:T(8,128)(2,1)} collective-permute-done((bf16[2,256,1024]{2,1,0:T(8,128)(2,1)}, bf16[2,256,1024]{2,1,0:T(8,128)(2,1)}, u32[]{:S(2)}, u32[]{:S(2)}) %collective-permute-start.1) | collective-permute-done | bytes 1048608 | tf_op jit(solution)/shard_map/ppermute | solution.py:20
  163.5 65.4 %collective-permute-done.2 = bf16[2,256,1024]{2,1,0:T(8,128)(2,1)} collective-permute-done((bf16[2,256,1024]{2,1,0:T(8,128)(2,1)}, bf16[2,256,1024]{2,1,0:T(8,128)(2,1)}, u32[]{:S(2)}, u32[]{:S(2)}) %collective-permute-start.2) | collective-permute-done | bytes 1048608 | tf_op jit(solution)/shard_map/ppermute | solution.py:20
  228.9 60.3 %collective-permute-start.7 = (bf16[2,256,1024]{2,1,0:T(8,128)(2,1)}, bf16[2,256,1024]{2,1,0:T(8,128)(2,1)S(1)}, u32[]{:S(2)}, u32[]{:S(2)}) collective-permute-start(bf16[2,256,1024]{2,1,0:T(8,128)(2,1)} %pad_maximum_fusion), channel_id=1, source_target_pairs={{0,4},{4,8},{8,12},{12,16},{16,20},{20,24},{24,28},{28,32},{32,36}... | collective-permute-start | bytes 3145736 | tf_op jit(solution)/shard_map/ppermute | solution.py:20
  289.2 2.3 constant_dynamic-update-slice_fusion.8
  293.8 2.3 constant_dynamic-update-slice_fusion.6
  296.1 2.3 constant_dynamic-update-slice_fusion.5
  298.4 9.0 %collective-permute-done.4 = bf16[2,256,1024]{2,1,0:T(8,128)(2,1)} collective-permute-done((bf16[2,256,1024]{2,1,0:T(8,128)(2,1)}, bf16[2,256,1024]{2,1,0:T(8,128)(2,1)}, u32[]{:S(2)}, u32[]{:S(2)}) %collective-permute-start.4) | collective-permute-done | bytes 1048608 | tf_op jit(solution)/shard_map/ppermute | solution.py:20
  307.4 2.3 constant_dynamic-update-slice_fusion.4
  309.7 79.5 %collective-permute-done.5 = bf16[2,256,1024]{2,1,0:T(8,128)(2,1)} collective-permute-done((bf16[2,256,1024]{2,1,0:T(8,128)(2,1)}, bf16[2,256,1024]{2,1,0:T(8,128)(2,1)}, u32[]{:S(2)}, u32[]{:S(2)}) %collective-permute-start.5) | collective-permute-done | bytes 1048608 | tf_op jit(solution)/shard_map/ppermute | solution.py:20
  391.5 25.0 %collective-permute-done.6 = bf16[2,256,1024]{2,1,0:T(8,128)(2,1)S(1)} collective-permute-done((bf16[2,256,1024]{2,1,0:T(8,128)(2,1)}, bf16[2,256,1024]{2,1,0:T(8,128)(2,1)S(1)}, u32[]{:S(2)}, u32[]{:S(2)}) %collective-permute-start.6) | collective-permute-done | bytes 1048608 | tf_op jit(solution)/shard_map/ppermute | solution.py:20
  417.6 14.0 %collective-permute-done.7 = bf16[2,256,1024]{2,1,0:T(8,128)(2,1)S(1)} collective-permute-done((bf16[2,256,1024]{2,1,0:T(8,128)(2,1)}, bf16[2,256,1024]{2,1,0:T(8,128)(2,1)S(1)}, u32[]{:S(2)}, u32[]{:S(2)}) %collective-permute-start.7) | collective-permute-done | bytes 1048608 | tf_op jit(solution)/shard_map/ppermute | solution.py:20
  433.7 7.1 %slice_bitcast_fusion = (bf16[2304,1024]{1,0:T(8,128)(2,1)}, bf16[2304,1024]{1,0:T(8,128)(2,1)S(1)}) fusion(bf16[2,2304,1024]{2,1,0:T(8,128)(2,1)} %constant_dynamic-update-slice_fusion), kind=kLoop, calls=%fused_computation.478 | loop fusion | bytes 18874368 | tf_op jit(solution)/shard_map/squeeze | solution.py:105
  444.7 2.5 fusion.200
  448.6 4.0 fusion.199
  462.9 38.6 %all-gather.6.cloned.1.call-done = f32[2048,1024]{1,0:T(8,128)} async-done(((f32[16,1024]{1,0:T(8,128)}), f32[2048,1024]{1,0:T(8,128)}) %all-gather.6.cloned.1.call-update) | async-done | bytes 8388624 | tf_op jit(solution)/shard_map/all_gather | solution.py:25
  501.5 119.9 %while.39 = (s32[]{:T(128)}, f32[16,1024]{1,0:T(8,128)S(1)}, s32[]{:T(128)}, f32[128,16,1024]{2,1,0:T(8,128)}, f32[128,16,1024]{2,1,0:T(8,128)}, /*index=5*/s32[]{:T(128)}, s32[]{:T(128)}) while((s32[]{:T(128)}, f32[16,1024]{1,0:T(8,128)S(1)}, s32[]{:T(128)}, f32[128,16,1024]{2,1,0:T(8,128)}, f32[128,16,1024]{2,1,0:T(8,128)}, ...), condition=%wide.region_21.22_spmd.clone, body=%wide.region_20.21_spmd.clone.sunk | while | flops 65540 | bytes 262245 | solution.py:37
  621.4 28.7 %while.37 = (s32[]{:T(128)}, f32[16,1024]{1,0:T(8,128)S(1)}, f32[8,32,1024]{2,1,0:T(8,128)}, f32[8,32,1024]{2,1,0:T(8,128)S(1)}, f32[16,1024]{1,0:T(8,128)S(1)},...) while((s32[]{:T(128)}, f32[16,1024]{1,0:T(8,128)S(1)}, ...), condition=%wide.region_55.56_spmd, body=%wide.region_22.55_spmd.sunk | while | flops 4718625 | bytes 3357861 | solution.py:69
  650.1 2.6 fusion.227
  (389 shorter events, 203.3 us)
Async XLA Ops:
  7.2 12.7 %copy-start = (bf16[256,1024]{1,0:T(8,128)(2,1)S(1)}, bf16[256,1024]{1,0:T(8,128)(2,1)}, u32[]{:S(2)}) copy-start(bf16[256,1024]{1,0:T(8,128)(2,1)} %param.24) | copy-start | bytes 1572868
  7.2 455.7 %all-gather.8.cloned.1.call-start = ((), (), s32[]{:S(2)}) async-start(), calls=%async_computation.1 | async-start | bytes 8454144 | tf_op jit(solution)/shard_map/all_gather | solution.py:25
  8.6 13.8 %copy-start.2 = (f32[16,1024]{1,0:T(8,128)S(1)}, f32[16,1024]{1,0:T(8,128)}, u32[]{:S(2)}) copy-start(f32[16,1024]{1,0:T(8,128)} %param.26) | copy-start | bytes 196612
  22.4 40.0 %copy-start.4 = (bf16[256,1024]{1,0:T(8,128)(2,1)S(1)}, bf16[256,1024]{1,0:T(8,128)(2,1)}, u32[]{:S(2)}) copy-start(bf16[256,1024]{1,0:T(8,128)(2,1)} %param.19) | copy-start | bytes 1572868
  22.4 40.0 %copy-start.5 = (bf16[256,1024]{1,0:T(8,128)(2,1)S(1)}, bf16[256,1024]{1,0:T(8,128)(2,1)}, u32[]{:S(2)}) copy-start(bf16[256,1024]{1,0:T(8,128)(2,1)} %param.18) | copy-start | bytes 1572868
  61.0 68.4 %copy-start.7 = (f32[256,16]{0,1:T(8,128)S(1)}, f32[256,16]{0,1:T(8,128)}, u32[]{:S(2)}) copy-start(f32[256,16]{0,1:T(8,128)} %get-tuple-element.566) | copy-start | bytes 49156
  61.0 440.5 %all-gather.6.cloned.1.call-start = ((), (), s32[]{:S(2)}) async-start(), calls=%async_computation | async-start | bytes 8454144 | tf_op jit(solution)/shard_map/all_gather | solution.py:25
  63.5 39.0 %collective-permute-start = (bf16[2,256,1024]{2,1,0:T(8,128)(2,1)}, bf16[2,256,1024]{2,1,0:T(8,128)(2,1)}, u32[]{:S(2)}, u32[]{:S(2)}) collective-permute-start(bf16[2,256,1024]{2,1,0:T(8,128)(2,1)} %pad_maximum_fusion), channel_id=1, source_target_pairs={{0,32},{4,36},{8,40},{12,44},{16,48},{20,52},{24,56},{28,60},{32,6... | collective-permute-start | bytes 3145736 | tf_op jit(solution)/shard_map/ppermute | solution.py:20
  72.0 90.1 %collective-permute-start.1 = (bf16[2,256,1024]{2,1,0:T(8,128)(2,1)}, bf16[2,256,1024]{2,1,0:T(8,128)(2,1)}, u32[]{:S(2)}, u32[]{:S(2)}) collective-permute-start(bf16[2,256,1024]{2,1,0:T(8,128)(2,1)} %pad_maximum_fusion), channel_id=1, source_target_pairs={{0,28},{4,32},{8,36},{12,40},{16,44},{20,48},{24,52},{28,56},{32,6... | collective-permute-start | bytes 3145736 | tf_op jit(solution)/shard_map/ppermute | solution.py:20
  79.3 149.7 %collective-permute-start.2 = (bf16[2,256,1024]{2,1,0:T(8,128)(2,1)}, bf16[2,256,1024]{2,1,0:T(8,128)(2,1)}, u32[]{:S(2)}, u32[]{:S(2)}) collective-permute-start(bf16[2,256,1024]{2,1,0:T(8,128)(2,1)} %pad_maximum_fusion), channel_id=1, source_target_pairs={{0,24},{4,28},{8,32},{12,36},{16,40},{20,44},{24,48},{28,52},{32,5... | collective-permute-start | bytes 3145736 | tf_op jit(solution)/shard_map/ppermute | solution.py:20
  84.5 211.6 %collective-permute-start.3 = (bf16[2,256,1024]{2,1,0:T(8,128)(2,1)}, bf16[2,256,1024]{2,1,0:T(8,128)(2,1)}, u32[]{:S(2)}, u32[]{:S(2)}) collective-permute-start(bf16[2,256,1024]{2,1,0:T(8,128)(2,1)} %pad_maximum_fusion), channel_id=1, source_target_pairs={{0,20},{4,24},{8,28},{12,32},{16,36},{20,40},{24,44},{28,48},{32,5... | collective-permute-start | bytes 3145736 | tf_op jit(solution)/shard_map/ppermute | solution.py:20
  86.8 220.6 %collective-permute-start.4 = (bf16[2,256,1024]{2,1,0:T(8,128)(2,1)}, bf16[2,256,1024]{2,1,0:T(8,128)(2,1)}, u32[]{:S(2)}, u32[]{:S(2)}) collective-permute-start(bf16[2,256,1024]{2,1,0:T(8,128)(2,1)} %pad_maximum_fusion), channel_id=1, source_target_pairs={{0,16},{4,20},{8,24},{12,28},{16,32},{20,36},{24,40},{28,44},{32,4... | collective-permute-start | bytes 3145736 | tf_op jit(solution)/shard_map/ppermute | solution.py:20
  102.6 286.7 %collective-permute-start.5 = (bf16[2,256,1024]{2,1,0:T(8,128)(2,1)}, bf16[2,256,1024]{2,1,0:T(8,128)(2,1)}, u32[]{:S(2)}, u32[]{:S(2)}) collective-permute-start(bf16[2,256,1024]{2,1,0:T(8,128)(2,1)} %pad_maximum_fusion), channel_id=1, source_target_pairs={{0,12},{4,16},{8,20},{12,24},{16,28},{20,32},{24,36},{28,40},{32,4... | collective-permute-start | bytes 3145736 | tf_op jit(solution)/shard_map/ppermute | solution.py:20
  162.1 254.4 %collective-permute-start.6 = (bf16[2,256,1024]{2,1,0:T(8,128)(2,1)}, bf16[2,256,1024]{2,1,0:T(8,128)(2,1)S(1)}, u32[]{:S(2)}, u32[]{:S(2)}) collective-permute-start(bf16[2,256,1024]{2,1,0:T(8,128)(2,1)} %pad_maximum_fusion), channel_id=1, source_target_pairs={{0,8},{4,12},{8,16},{12,20},{16,24},{20,28},{24,32},{28,36},{32,40... | collective-permute-start | bytes 3145736 | tf_op jit(solution)/shard_map/ppermute | solution.py:20
  228.9 202.6 %collective-permute-start.7 = (bf16[2,256,1024]{2,1,0:T(8,128)(2,1)}, bf16[2,256,1024]{2,1,0:T(8,128)(2,1)S(1)}, u32[]{:S(2)}, u32[]{:S(2)}) collective-permute-start(bf16[2,256,1024]{2,1,0:T(8,128)(2,1)} %pad_maximum_fusion), channel_id=1, source_target_pairs={{0,4},{4,8},{8,12},{12,16},{16,20},{20,24},{24,28},{28,32},{32,36}... | collective-permute-start | bytes 3145736 | tf_op jit(solution)/shard_map/ppermute | solution.py:20
  433.7 7.1 %copy-start.6 = (bf16[256,1024]{1,0:T(8,128)(2,1)S(1)}, bf16[256,1024]{1,0:T(8,128)(2,1)}, u32[]{:S(2)}) copy-start(bf16[256,1024]{1,0:T(8,128)(2,1)} %param.17) | copy-start | bytes 1572868
  443.7 3.6 slice-start
  444.7 2.5 slice-start.1
  621.4 28.7 %copy-start.3 = (bf16[256,1024]{1,0:T(8,128)(2,1)S(1)}, bf16[256,1024]{1,0:T(8,128)(2,1)}, u32[]{:S(2)}) copy-start(bf16[256,1024]{1,0:T(8,128)(2,1)} %param.20) | copy-start | bytes 1572868
  621.4 28.7 %copy-start.8 = (f32[1024]{0:T(1024)S(1)}, f32[1024]{0:T(1024)}, u32[]{:S(2)}) copy-start(f32[1024]{0:T(1024)} %param.27) | copy-start | bytes 12292
  650.1 2.6 copy-start.1
Sparse Core Ops, SparseCore 0:
  61.1 345.5 all-gather.7
  409.8 91.6 all-gather.5
